TPU v7x, 32 devices: a whole 2x2x4 slice. The times are simulated.
32 devices in a mesh: row: 8 (over z, y), col: 4 (over x, core).
Axes of the slice: x: 2, y: 2, z: 4, core: 2. Of those that a mesh axis runs over, the one named last changes fastest.
Arguments:
- orbitals: bfloat16 [20480, 384], P(('row', 'col')), may hold values from -6 to 6
- coulomb: float32 [20480, 20480], P('row', 'col'), may hold values from -0.001953125 to 0.001953125
- interp: bfloat16 [4096, 20480], P('row', 'col'), may hold values from -0.0390625 to 0.0390625
Outputs:
- exchanged: bfloat16 [4096, 384], P(('row', 'col'))
All inputs are finite; a program needn't handle non-finite values.
Results may differ from a plain program's by a relative error of at most 0.018.
Values may be sent and summed in bfloat16 or wider, within the bound.
No kernel may reach another device: no remote copies, remote signals or barrier semaphores. Data moves between devices by JAX's collectives and lax.ppermute only.
A program may use at most 128 MiB of HBM per device.

v0:
```python
import functools

import jax
import jax.numpy as jnp
from jax import lax
from jax.experimental import pallas as pl
from jax.experimental.pallas import tpu as pltpu
from jax.sharding import PartitionSpec as P


AXES = ("row", "col")
NT = (((1,), (1,)), ((), ()))
TN = (((0,), (0,)), ((), ()))


def plan(rows, cols):
    factor = rows // cols
    half = max(cols // 2, 1)

    def turn(c, target):
        return (c & 1) * half | ((c >> 1) ^ (target & (1 if half > 1 else 0)))

    ring = []
    for y in range(factor):
        zs = range(cols) if y % 2 == 0 else reversed(range(cols))
        ring += [z * factor + y for z in zs]
    position = {row: p for p, row in enumerate(ring)}

    deal, hop, table = [], [], []
    for row in range(rows):
        z, y = divmod(row, factor)
        for c in range(cols):
            deal.append((row * cols + c, (turn(c, z) * factor + y) * cols + z))
    for row in range(rows):
        p = position[row]
        table.append([])
        for c in range(cols):
            back = {turn(s, c): s for s in range(cols)}
            piece = [(r % factor) * cols + back[r // factor] for r in ring]
            step = 1 if c % 2 == 0 else -1
            hop.append((row * cols + c, ring[(p + step) % rows] * cols + c))
            passing = [piece[(p - step * k) % rows] for k in range(rows)]
            table[-1].append(passing + [c ^ mask for mask in range(cols)])

    def swap(bit):
        return [(r * cols + c, r * cols + (c ^ bit)) for r in range(rows) for c in range(cols)]

    return deal, hop, swap, table


def accumulate(near, far_ref, coulomb_ref, out_ref):
    @pl.when(pl.program_id(0) == 0)
    def _():
        out_ref[...] = jnp.zeros_like(out_ref)

    density = lax.dot_general(near, far_ref[...], NT, preferred_element_type=jnp.float32)
    weighted = (coulomb_ref[...] * density).astype(jnp.bfloat16)
    out_ref[...] += lax.dot_general(near, weighted, TN, preferred_element_type=jnp.float32)


def first_kernel(count, where, *refs):
    shards, (far_ref, coulomb_ref, out_ref, near_ref) = refs[:count], refs[count:]
    share = shards[0].shape[0]
    for q in range(count):

        @pl.when(pl.program_id(0) == q)
        def _():
            near_ref[q * share : (q + 1) * share, :] = shards[q][...]

    rows = pl.ds(pl.multiple_of(pl.program_id(0) * share, share), share)
    accumulate(near_ref[rows, :], far_ref, coulomb_ref, out_ref)


def next_kernel(where, near_ref, far_ref, coulomb_ref, out_ref):
    accumulate(near_ref[...], far_ref, coulomb_ref, out_ref)


def partial_of(k, where, near, far, coulomb):
    first = isinstance(near, list)
    count = len(near) if first else near.shape[0] // far.shape[0]
    share, norb = far.shape
    rows = where.shape[0] - count
    if share % 128:
        if first:
            near = jnp.concatenate(near, 0)
        column = lax.dynamic_slice_in_dim(coulomb, where[k] * share, share, 1)
        column = jnp.take(column.reshape(count, share, share), where[rows:], axis=0)
        density = lax.dot_general(near, far, NT, preferred_element_type=jnp.float32)
        weighted = (column.reshape(-1, share) * density).astype(jnp.bfloat16)
        return lax.dot_general(near, weighted, TN, preferred_element_type=jnp.float32), near

    fixed = lambda i, w: (0, 0)
    sums = jax.ShapeDtypeStruct((norb, share), jnp.float32)
    sums_spec = pl.BlockSpec((norb, share), fixed)
    shard_spec = pl.BlockSpec((share, norb), fixed)
    tail_specs = [shard_spec, pl.BlockSpec((share, share), lambda i, w: (w[rows + i], w[k]))]
    m = count * share
    options = dict(
        compiler_params=pltpu.CompilerParams(vmem_limit_bytes=20 << 20),
        cost_estimate=pl.CostEstimate(
            flops=4 * m * norb * share, bytes_accessed=4 * m * share, transcendentals=0
        ),
        name="partial",
    )
    if first:
        return pl.pallas_call(
            functools.partial(first_kernel, count),
            out_shape=(sums, jax.ShapeDtypeStruct((m, norb), jnp.bfloat16)),
            grid_spec=pltpu.PrefetchScalarGridSpec(
                num_scalar_prefetch=1,
                grid=(count,),
                in_specs=[shard_spec] * count + tail_specs,
                out_specs=(sums_spec, pl.BlockSpec((m, norb), fixed)),
            ),
            **options,
        )(where, pltpu.with_memory_space_constraint(near[0], pltpu.HBM), *near[1:], far, coulomb)
    return pl.pallas_call(
        next_kernel,
        out_shape=sums,
        grid_spec=pltpu.PrefetchScalarGridSpec(
            num_scalar_prefetch=1,
            grid=(count,),
            in_specs=[pl.BlockSpec((share, norb), lambda i, w: (i, 0))] + tail_specs,
            out_specs=sums_spec,
        ),
        **options,
    )(where, near, far, coulomb), near


def term_kernel(k, rows, where, interp_ref, upper_ref, lower_ref, *refs):
    refs, sems = list(refs[:-1]), refs[-1]
    share = upper_ref.shape[1]

    def fetch(step, to, sem):
        columns = pl.ds(pl.multiple_of(where[(step - 1) % rows] * share, share), share)
        return pltpu.make_async_copy(interp_ref.at[:, columns], to, sem)

    before = refs.pop(0) if k else None
    block_ref = refs.pop(0) if k else refs.pop()
    out_ref = refs[0]
    copies = [] if k else [fetch(k, block_ref, sems.at[0])]
    if k < rows - 1:
        copies.append(fetch(k + 1, refs[1], sems.at[1]))
    for copy in copies:
        copy.start()
    if not k:
        copies.pop(0).wait()
    piece = jnp.concatenate([upper_ref[...], lower_ref[...]], 0)
    term = lax.dot_general(block_ref[...], piece, NT, preferred_element_type=jnp.float32)
    out_ref[...] = before[...] + term if k else term
    for copy in copies:
        copy.wait()


def term_of(k, rows, where, interp, upper, lower, total, block):
    g = interp.shape[0]
    share = upper.shape[1]
    norb = upper.shape[0] + lower.shape[0]
    last = k == rows - 1
    if share % 128:
        block = lax.dynamic_slice_in_dim(interp, where[(k - 1) % rows] * share, share, 1)
        piece = jnp.concatenate([upper, lower], 0)
        term = lax.dot_general(block, piece, NT, preferred_element_type=jnp.float32)
        return (total + term if k else term), None
    vmem = pl.BlockSpec(memory_space=pltpu.VMEM)
    sums = jax.ShapeDtypeStruct((g, norb), jnp.float32)
    columns = jax.ShapeDtypeStruct((g, share), interp.dtype)
    carried = [total, block] if k else []
    out = pl.pallas_call(
        functools.partial(term_kernel, k, rows),
        out_shape=(sums,) if last else (sums, columns),
        in_specs=[pl.BlockSpec(memory_space=pltpu.SMEM), pl.BlockSpec(memory_space=pltpu.HBM)]
        + [vmem] * (2 + len(carried)),
        out_specs=(vmem,) if last else (vmem, vmem),
        scratch_shapes=([] if k else [pltpu.VMEM(columns.shape, columns.dtype)])
        + [pltpu.SemaphoreType.DMA((2,))],
        compiler_params=pltpu.CompilerParams(vmem_limit_bytes=8 << 20),
        cost_estimate=pl.CostEstimate(
            flops=2 * g * norb * share, bytes_accessed=2 * g * share, transcendentals=0
        ),
        name="term",
    )(where, pltpu.with_memory_space_constraint(interp, pltpu.HBM), upper, lower, *carried)
    return out if len(out) == 2 else (out[0], None)


def local(rows, cols, orbitals, coulomb, interp):
    deal, hop, swap, table = plan(rows, cols)
    _, norb = orbitals.shape
    row, col = lax.axis_index("row"), lax.axis_index("col")
    table = jnp.asarray(table, jnp.int32)
    where = lax.dynamic_slice(table, (row, col, 0), (1, 1, rows + cols)).reshape(rows + cols)

    far = lax.ppermute(orbitals, AXES, deal)
    held = [(0, orbitals)]
    bit = cols // 2
    while bit:
        for mask, block in list(held):
            held.append((mask ^ bit, lax.ppermute(block, AXES, swap(bit))))
        bit //= 2
    near = [block for mask, block in sorted(held, key=lambda item: item[0])]

    sent = None
    for k in range(rows):
        following = lax.ppermute(far, AXES, hop) if k < rows - 1 else None
        part, near = partial_of(k, where, near, far, coulomb)
        if sent is not None:
            part = part + lax.ppermute(sent, AXES, hop).astype(jnp.float32)
        sent = part.astype(jnp.bfloat16)
        far = following

    cut = norb // 32 * 16
    upper, lower, total, block = sent[:cut], sent[cut:], None, None
    for k in range(rows):
        if total is not None:
            upper, total = lax.optimization_barrier((upper, total))
        if k < rows - 1:
            after = lax.ppermute(upper, AXES, hop), lax.ppermute(lower, AXES, hop)
        total, block = term_of(k, rows, where, interp, upper, lower, total, block)
        upper, lower = after

    bit, blocks = 1, cols
    while bit < cols:
        pairs = total.reshape(blocks // 2, 2, -1, norb)
        mine = (col // bit) % 2
        keep = lax.dynamic_index_in_dim(pairs, mine, 1, keepdims=False)
        give = lax.dynamic_index_in_dim(pairs, 1 - mine, 1, keepdims=False)
        total = keep + lax.ppermute(give.astype(jnp.bfloat16), AXES, swap(bit)).astype(jnp.float32)
        bit, blocks = bit * 2, blocks // 2
    return total.reshape(-1, norb).astype(jnp.bfloat16)


def solution(mesh):
    in_specs = (P(("row", "col"), None), P("row", "col"), P("row", "col"))
    out_specs = P(("row", "col"), None)
    rows, cols = mesh.shape["row"], mesh.shape["col"]

    def body(*args):
        return local(rows, cols, *args)

    return jax.shard_map(body, mesh=mesh, in_specs=in_specs, out_specs=out_specs, check_vma=False)
```

profile of v0, /device:TPU:0, one launch (start us, length us, event | category | flops | bytes accessed | tf_op | source)
XLA Modules:
  0.0 161.6 jit_solution(13928096524313712271)
XLA Ops:
  0.0 3.0 %collective-permute-start.1 = (bf16[640,384]{1,0:T(8,128)(2,1)}, bf16[640,384]{1,0:T(8,128)(2,1)S(1)}, u32[]{:S(2)}, u32[]{:S(2)}) collective-permute-start(bf16[640,384]{1,0:T(8,128)(2,1)} %refs_0_.1), channel_id=1, source_target_pairs={{0,2},{1,3},{2,0},{3,1},{4,6},{5,7},{6,4},{7,5},{8,10},{9,11},{10,... | collective-permute-start | bytes 1474568 | tf_op jit(solution)/shard_map/ppermute | solution.py:198
  3.0 1.7 %collective-permute-start.3 = (bf16[640,384]{1,0:T(8,128)(2,1)}, bf16[640,384]{1,0:T(8,128)(2,1)S(1)}, u32[]{:S(2)}, u32[]{:S(2)}) collective-permute-start(bf16[640,384]{1,0:T(8,128)(2,1)} %refs_0_.1), channel_id=1, source_target_pairs={{0,0},{1,16},{2,8},{3,24},{4,4},{5,20},{6,12},{7,28},{8,9},{9,25},... | collective-permute-start | bytes 1474568 | tf_op jit(solution)/shard_map/ppermute | solution.py:193
  4.6 3.0 %collective-permute-start = (bf16[640,384]{1,0:T(8,128)(2,1)}, bf16[640,384]{1,0:T(8,128)(2,1)S(1)}, u32[]{:S(2)}, u32[]{:S(2)}) collective-permute-start(bf16[640,384]{1,0:T(8,128)(2,1)} %refs_0_.1), channel_id=1, source_target_pairs={{0,1},{1,0},{2,3},{3,2},{4,5},{5,4},{6,7},{7,6},{8,9},{9,8},{10,11... | collective-permute-start | bytes 1474568 | tf_op jit(solution)/shard_map/ppermute | solution.py:198
  7.6 12.0 %collective-permute-done.1.refs_2_ = bf16[640,384]{1,0:T(8,128)(2,1)S(1)} collective-permute-done((bf16[640,384]{1,0:T(8,128)(2,1)}, bf16[640,384]{1,0:T(8,128)(2,1)S(1)}, u32[]{:S(2)}, u32[]{:S(2)}) %collective-permute-start.1) | collective-permute-done | bytes 491552 | tf_op jit(solution)/shard_map/ppermute | solution.py:198
  20.4 1.8 %collective-permute-start.4 = (bf16[640,384]{1,0:T(8,128)(2,1)S(1)}, bf16[640,384]{1,0:T(8,128)(2,1)S(1)}, u32[]{:S(2)}, u32[]{:S(2)}) collective-permute-start(bf16[640,384]{1,0:T(8,128)(2,1)S(1)} %collective-permute-done.3.refs_4_), channel_id=1, source_target_pairs={{0,8},{1,5},{2,10},{3,7},{4,0},{5,13},{6,2},{7,15},{8,16},{9,1},{1... | collective-permute-start | bytes 1474568 | tf_op jit(solution)/shard_map/ppermute | solution.py:204
  22.2 7.3 %partial.8 = (f32[384,640]{1,0:T(8,128)S(1)}, bf16[2560,384]{1,0:T(8,128)(2,1)S(1)}) custom-call(s32[12]{0:T(128)S(1)} %fusion.2.where, bf16[640,384]{1,0:T(8,128)(2,1)} %refs_0_.1, bf16[640,384]{1,0:T(8,128)(2,1)S(1)} %collective-permute-done.refs_1_, bf16[640,384]{1,0:T(8,128)(2,1)S(1)} %collective-permute-done.1.refs_2_, ...), custom_call_target="tpu_custom_call" | custom-call | flops 2516582400 | bytes 6553600 | tf_op jit(solution)/shard_map/partial/pallas_call | solution.py:106
  29.5 1.6 %collective-permute-start.11 = (bf16[384,640]{1,0:T(8,128)(2,1)S(1)}, bf16[384,640]{1,0:T(8,128)(2,1)S(1)}, u32[]{:S(2)}, u32[]{:S(2)}) collective-permute-start(bf16[384,640]{1,0:T(8,128)(2,1)S(1)} %convert_element_type.68), channel_id=1, source_target_pairs={{0,8},{1,5},{2,10},{3,7},{4,0},{5,13},{6,2},{7,15},{8,16},{9,1},{1... | collective-permute-start | bytes 1474568 | tf_op jit(solution)/shard_map/ppermute | solution.py:207
  32.8 7.0 %partial.15 = f32[384,640]{1,0:T(8,128)S(1)} custom-call(s32[12]{0:T(128)S(1)} %fusion.2.where, bf16[2560,384]{1,0:T(8,128)(2,1)S(1)} %get-tuple-element.35.near_ref, bf16[640,384]{1,0:T(8,128)(2,1)S(1)} %collective-permute-done.4.far_ref, f32[2560,5120]{1,0:T(8,128)} %coulomb_ref.13), custom_call_target="tpu_custom_call" | custom-call | flops 2516582400 | bytes 6553600 | tf_op jit(solution)/shard_map/partial/pallas_call | solution.py:117
  41.5 2.2 %collective-permute-done.5.far_ref = bf16[640,384]{1,0:T(8,128)(2,1)S(1)} collective-permute-done((bf16[640,384]{1,0:T(8,128)(2,1)S(1)}, bf16[640,384]{1,0:T(8,128)(2,1)S(1)}, u32[]{:S(2)}, u32[]{:S(2)}) %collective-permute-start.5) | collective-permute-done | bytes 491552 | tf_op jit(solution)/shard_map/ppermute | solution.py:204
  43.7 1.6 collective-permute-start.6
  45.3 7.0 %partial.14 = f32[384,640]{1,0:T(8,128)S(1)} custom-call(s32[12]{0:T(128)S(1)} %fusion.2.where, bf16[2560,384]{1,0:T(8,128)(2,1)S(1)} %get-tuple-element.35.near_ref, bf16[640,384]{1,0:T(8,128)(2,1)S(1)} %collective-permute-done.5.far_ref, f32[2560,5120]{1,0:T(8,128)} %coulomb_ref.13), custom_call_target="tpu_custom_call" | custom-call | flops 2516582400 | bytes 6553600 | tf_op jit(solution)/shard_map/partial/pallas_call | solution.py:117
  52.4 1.6 %collective-permute-start.13 = (bf16[384,640]{1,0:T(8,128)(2,1)S(1)}, bf16[384,640]{1,0:T(8,128)(2,1)S(1)}, u32[]{:S(2)}, u32[]{:S(2)}) collective-permute-start(bf16[384,640]{1,0:T(8,128)(2,1)S(1)} %add_convert_fusion.5), channel_id=1, source_target_pairs={{0,8},{1,5},{2,10},{3,7},{4,0},{5,13},{6,2},{7,15},{8,16},{9,1},{1... | collective-permute-start | bytes 1474568 | tf_op jit(solution)/shard_map/ppermute | solution.py:207
  54.2 1.6 collective-permute-start.7
  55.8 7.0 %partial.13 = f32[384,640]{1,0:T(8,128)S(1)} custom-call(s32[12]{0:T(128)S(1)} %fusion.2.where, bf16[2560,384]{1,0:T(8,128)(2,1)S(1)} %get-tuple-element.35.near_ref, bf16[640,384]{1,0:T(8,128)(2,1)S(1)} %collective-permute-done.6.far_ref, f32[2560,5120]{1,0:T(8,128)} %coulomb_ref.13), custom_call_target="tpu_custom_call" | custom-call | flops 2516582400 | bytes 6553600 | tf_op jit(solution)/shard_map/partial/pallas_call | solution.py:117
  62.9 1.6 %collective-permute-start.14 = (bf16[384,640]{1,0:T(8,128)(2,1)S(1)}, bf16[384,640]{1,0:T(8,128)(2,1)S(1)}, u32[]{:S(2)}, u32[]{:S(2)}) collective-permute-start(bf16[384,640]{1,0:T(8,128)(2,1)S(1)} %add_convert_fusion.4), channel_id=1, source_target_pairs={{0,8},{1,5},{2,10},{3,7},{4,0},{5,13},{6,2},{7,15},{8,16},{9,1},{1... | collective-permute-start | bytes 1474568 | tf_op jit(solution)/shard_map/ppermute | solution.py:207
  64.6 2.0 %collective-permute-done.7.far_ref = bf16[640,384]{1,0:T(8,128)(2,1)S(1)} collective-permute-done((bf16[640,384]{1,0:T(8,128)(2,1)S(1)}, bf16[640,384]{1,0:T(8,128)(2,1)S(1)}, u32[]{:S(2)}, u32[]{:S(2)}) %collective-permute-start.7) | collective-permute-done | bytes 491552 | tf_op jit(solution)/shard_map/ppermute | solution.py:204
  68.1 7.0 %partial.12 = f32[384,640]{1,0:T(8,128)S(1)} custom-call(s32[12]{0:T(128)S(1)} %fusion.2.where, bf16[2560,384]{1,0:T(8,128)(2,1)S(1)} %get-tuple-element.35.near_ref, bf16[640,384]{1,0:T(8,128)(2,1)S(1)} %collective-permute-done.7.far_ref, f32[2560,5120]{1,0:T(8,128)} %coulomb_ref.13), custom_call_target="tpu_custom_call" | custom-call | flops 2516582400 | bytes 6553600 | tf_op jit(solution)/shard_map/partial/pallas_call | solution.py:117
  75.3 1.6 collective-permute-start.15
  78.7 7.0 %partial.11 = f32[384,640]{1,0:T(8,128)S(1)} custom-call(s32[12]{0:T(128)S(1)} %fusion.2.where, bf16[2560,384]{1,0:T(8,128)(2,1)S(1)} %get-tuple-element.35.near_ref, bf16[640,384]{1,0:T(8,128)(2,1)S(1)} %collective-permute-done.8.far_ref, f32[2560,5120]{1,0:T(8,128)} %coulomb_ref.13), custom_call_target="tpu_custom_call" | custom-call | flops 2516582400 | bytes 6553600 | tf_op jit(solution)/shard_map/partial/pallas_call | solution.py:117
  85.8 1.6 collective-permute-start.16
  87.4 2.0 %collective-permute-done.9.far_ref = bf16[640,384]{1,0:T(8,128)(2,1)S(1)} collective-permute-done((bf16[640,384]{1,0:T(8,128)(2,1)S(1)}, bf16[640,384]{1,0:T(8,128)(2,1)S(1)}, u32[]{:S(2)}, u32[]{:S(2)}) %collective-permute-start.9) | collective-permute-done | bytes 491552 | tf_op jit(solution)/shard_map/ppermute | solution.py:204
  90.9 7.0 %partial.10 = f32[384,640]{1,0:T(8,128)S(1)} custom-call(s32[12]{0:T(128)S(1)} %fusion.2.where, bf16[2560,384]{1,0:T(8,128)(2,1)S(1)} %get-tuple-element.35.near_ref, bf16[640,384]{1,0:T(8,128)(2,1)S(1)} %collective-permute-done.9.far_ref, f32[2560,5120]{1,0:T(8,128)} %coulomb_ref.13), custom_call_target="tpu_custom_call" | custom-call | flops 2516582400 | bytes 6553600 | tf_op jit(solution)/shard_map/partial/pallas_call | solution.py:117
  100.0 7.0 %partial.9 = f32[384,640]{1,0:T(8,128)S(1)} custom-call(s32[12]{0:T(128)S(1)} %fusion.2.where, bf16[2560,384]{1,0:T(8,128)(2,1)S(1)} %get-tuple-element.35.near_ref, bf16[640,384]{1,0:T(8,128)(2,1)S(1)} %collective-permute-done.10.far_ref, f32[2560,5120]{1,0:T(8,128)} %coulomb_ref.13), custom_call_target="tpu_custom_call" | custom-call | flops 2516582400 | bytes 6553600 | tf_op jit(solution)/shard_map/partial/pallas_call | solution.py:117
  109.9 2.2 %term.8 = (f32[512,384]{1,0:T(8,128)S(1)}, bf16[512,640]{1,0:T(8,128)(2,1)S(1)}) custom-call(s32[12]{0:T(128)S(1)} %fusion.2.where, bf16[512,5120]{1,0:T(8,128)(2,1)} %interp_ref.15, bf16[192,640]{1,0:T(8,128)(2,1)S(1)} %get-tuple-element.66.upper_ref, bf16[192,640]{1,0:T(8,128)(2,1)S(1)} %get-tuple-element.65.lower_ref), custom_call_target="tpu_custom_call" | custom-call | flops 251658240 | bytes 655360 | tf_op jit(solution)/shard_map/term/pallas_call | solution.py:169
  117.6 2.1 %term.9 = (f32[512,384]{1,0:T(8,128)S(1)}, bf16[512,640]{1,0:T(8,128)(2,1)S(1)}) custom-call(s32[12]{0:T(128)S(1)} %fusion.2.where, bf16[512,5120]{1,0:T(8,128)(2,1)} %interp_ref.15, bf16[192,640]{1,0:T(8,128)(2,1)S(1)} %collective-permute-done.18.upper_ref, bf16[192,640]{1,0:T(8,128)(2,1)S(1)} %collective-permute-done.20.lower_ref, ...), custom_call_target="tpu_custom_call" | custom-call | flops 251658240 | bytes 655360 | tf_op jit(solution)/shard_map/term/pallas_call | solution.py:169
  123.7 2.1 %term.10 = (f32[512,384]{1,0:T(8,128)S(1)}, bf16[512,640]{1,0:T(8,128)(2,1)S(1)}) custom-call(s32[12]{0:T(128)S(1)} %fusion.2.where, bf16[512,5120]{1,0:T(8,128)(2,1)} %interp_ref.15, bf16[192,640]{1,0:T(8,128)(2,1)S(1)} %collective-permute-done.19.upper_ref, bf16[192,640]{1,0:T(8,128)(2,1)S(1)} %collective-permute-done.22.lower_ref, ...), custom_call_target="tpu_custom_call" | custom-call | flops 251658240 | bytes 655360 | tf_op jit(solution)/shard_map/term/pallas_call | solution.py:169
  129.9 2.1 %term.11 = (f32[512,384]{1,0:T(8,128)S(1)}, bf16[512,640]{1,0:T(8,128)(2,1)S(1)}) custom-call(s32[12]{0:T(128)S(1)} %fusion.2.where, bf16[512,5120]{1,0:T(8,128)(2,1)} %interp_ref.15, bf16[192,640]{1,0:T(8,128)(2,1)S(1)} %collective-permute-done.21.upper_ref, bf16[192,640]{1,0:T(8,128)(2,1)S(1)} %collective-permute-done.24.lower_ref, ...), custom_call_target="tpu_custom_call" | custom-call | flops 251658240 | bytes 655360 | tf_op jit(solution)/shard_map/term/pallas_call | solution.py:169
  136.1 2.1 %term.12 = (f32[512,384]{1,0:T(8,128)S(1)}, bf16[512,640]{1,0:T(8,128)(2,1)S(1)}) custom-call(s32[12]{0:T(128)S(1)} %fusion.2.where, bf16[512,5120]{1,0:T(8,128)(2,1)} %interp_ref.15, bf16[192,640]{1,0:T(8,128)(2,1)S(1)} %collective-permute-done.23.upper_ref, bf16[192,640]{1,0:T(8,128)(2,1)S(1)} %collective-permute-done.26.lower_ref, ...), custom_call_target="tpu_custom_call" | custom-call | flops 251658240 | bytes 655360 | tf_op jit(solution)/shard_map/term/pallas_call | solution.py:169
  142.3 2.1 %term.13 = (f32[512,384]{1,0:T(8,128)S(1)}, bf16[512,640]{1,0:T(8,128)(2,1)S(1)}) custom-call(s32[12]{0:T(128)S(1)} %fusion.2.where, bf16[512,5120]{1,0:T(8,128)(2,1)} %interp_ref.15, bf16[192,640]{1,0:T(8,128)(2,1)S(1)} %collective-permute-done.25.upper_ref, bf16[192,640]{1,0:T(8,128)(2,1)S(1)} %collective-permute-done.28.lower_ref, ...), custom_call_target="tpu_custom_call" | custom-call | flops 251658240 | bytes 655360 | tf_op jit(solution)/shard_map/term/pallas_call | solution.py:169
  148.5 2.1 %term.14 = (f32[512,384]{1,0:T(8,128)S(1)}, bf16[512,640]{1,0:T(8,128)(2,1)S(1)}) custom-call(s32[12]{0:T(128)S(1)} %fusion.2.where, bf16[512,5120]{1,0:T(8,128)(2,1)} %interp_ref.15, bf16[192,640]{1,0:T(8,128)(2,1)S(1)} %collective-permute-done.27.upper_ref, bf16[192,640]{1,0:T(8,128)(2,1)S(1)} %collective-permute-done.30.lower_ref, ...), custom_call_target="tpu_custom_call" | custom-call | flops 251658240 | bytes 655360 | tf_op jit(solution)/shard_map/term/pallas_call | solution.py:169
  150.7 2.6 %collective-permute-done.31.lower_ref = bf16[192,640]{1,0:T(8,128)(2,1)S(1)} collective-permute-done((bf16[192,640]{1,0:T(8,128)(2,1)S(1)}, bf16[192,640]{1,0:T(8,128)(2,1)S(1)}, u32[]{:S(2)}, u32[]{:S(2)}) %collective-permute-start.31) | collective-permute-done | bytes 245792 | tf_op jit(solution)/shard_map/ppermute | solution.py:217
  156.1 4.8 %collective-permute-done.33 = bf16[1,128,384]{2,1,0:T(8,128)(2,1)S(1)} collective-permute-done((bf16[1,128,384]{2,1,0:T(8,128)(2,1)S(1)}, bf16[1,128,384]{2,1,0:T(8,128)(2,1)S(1)}, u32[]{:S(2)}, u32[]{:S(2)}) %collective-permute-start.33) | collective-permute-done | bytes 98336 | tf_op jit(solution)/shard_map/ppermute | solution.py:227
  (66 shorter events, 43.9 us)
Async XLA Ops:
  0.0 19.7 %collective-permute-start.1 = (bf16[640,384]{1,0:T(8,128)(2,1)}, bf16[640,384]{1,0:T(8,128)(2,1)S(1)}, u32[]{:S(2)}, u32[]{:S(2)}) collective-permute-start(bf16[640,384]{1,0:T(8,128)(2,1)} %refs_0_.1), channel_id=1, source_target_pairs={{0,2},{1,3},{2,0},{3,1},{4,6},{5,7},{6,4},{7,5},{8,10},{9,11},{10,... | collective-permute-start | bytes 1474568 | tf_op jit(solution)/shard_map/ppermute | solution.py:198
  3.0 17.4 %collective-permute-start.3 = (bf16[640,384]{1,0:T(8,128)(2,1)}, bf16[640,384]{1,0:T(8,128)(2,1)S(1)}, u32[]{:S(2)}, u32[]{:S(2)}) collective-permute-start(bf16[640,384]{1,0:T(8,128)(2,1)} %refs_0_.1), channel_id=1, source_target_pairs={{0,0},{1,16},{2,8},{3,24},{4,4},{5,20},{6,12},{7,28},{8,9},{9,25},... | collective-permute-start | bytes 1474568 | tf_op jit(solution)/shard_map/ppermute | solution.py:193
  4.6 17.5 %collective-permute-start = (bf16[640,384]{1,0:T(8,128)(2,1)}, bf16[640,384]{1,0:T(8,128)(2,1)S(1)}, u32[]{:S(2)}, u32[]{:S(2)}) collective-permute-start(bf16[640,384]{1,0:T(8,128)(2,1)} %refs_0_.1), channel_id=1, source_target_pairs={{0,1},{1,0},{2,3},{3,2},{4,5},{5,4},{6,7},{7,6},{8,9},{9,8},{10,11... | collective-permute-start | bytes 1474568 | tf_op jit(solution)/shard_map/ppermute | solution.py:198
  20.4 10.8 %collective-permute-start.4 = (bf16[640,384]{1,0:T(8,128)(2,1)S(1)}, bf16[640,384]{1,0:T(8,128)(2,1)S(1)}, u32[]{:S(2)}, u32[]{:S(2)}) collective-permute-start(bf16[640,384]{1,0:T(8,128)(2,1)S(1)} %collective-permute-done.3.refs_4_), channel_id=1, source_target_pairs={{0,8},{1,5},{2,10},{3,7},{4,0},{5,13},{6,2},{7,15},{8,16},{9,1},{1... | collective-permute-start | bytes 1474568 | tf_op jit(solution)/shard_map/ppermute | solution.py:204
  29.5 10.2 %collective-permute-start.11 = (bf16[384,640]{1,0:T(8,128)(2,1)S(1)}, bf16[384,640]{1,0:T(8,128)(2,1)S(1)}, u32[]{:S(2)}, u32[]{:S(2)}) collective-permute-start(bf16[384,640]{1,0:T(8,128)(2,1)S(1)} %convert_element_type.68), channel_id=1, source_target_pairs={{0,8},{1,5},{2,10},{3,7},{4,0},{5,13},{6,2},{7,15},{8,16},{9,1},{1... | collective-permute-start | bytes 1474568 | tf_op jit(solution)/shard_map/ppermute | solution.py:207
  31.2 12.5 %collective-permute-start.5 = (bf16[640,384]{1,0:T(8,128)(2,1)S(1)}, bf16[640,384]{1,0:T(8,128)(2,1)S(1)}, u32[]{:S(2)}, u32[]{:S(2)}) collective-permute-start(bf16[640,384]{1,0:T(8,128)(2,1)S(1)} %collective-permute-done.4.far_ref), channel_id=1, source_target_pairs={{0,8},{1,5},{2,10},{3,7},{4,0},{5,13},{6,2},{7,15},{8,16},{9,1},{1... | collective-permute-start | bytes 1474568 | tf_op jit(solution)/shard_map/ppermute | solution.py:204
  39.9 12.4 %collective-permute-start.12 = (bf16[384,640]{1,0:T(8,128)(2,1)S(1)}, bf16[384,640]{1,0:T(8,128)(2,1)S(1)}, u32[]{:S(2)}, u32[]{:S(2)}) collective-permute-start(bf16[384,640]{1,0:T(8,128)(2,1)S(1)} %add_convert_fusion.6), channel_id=1, source_target_pairs={{0,8},{1,5},{2,10},{3,7},{4,0},{5,13},{6,2},{7,15},{8,16},{9,1},{1... | collective-permute-start | bytes 1474568 | tf_op jit(solution)/shard_map/ppermute | solution.py:207
  43.7 10.5 %collective-permute-start.6 = (bf16[640,384]{1,0:T(8,128)(2,1)S(1)}, bf16[640,384]{1,0:T(8,128)(2,1)S(1)}, u32[]{:S(2)}, u32[]{:S(2)}) collective-permute-start(bf16[640,384]{1,0:T(8,128)(2,1)S(1)} %collective-permute-done.5.far_ref), channel_id=1, source_target_pairs={{0,8},{1,5},{2,10},{3,7},{4,0},{5,13},{6,2},{7,15},{8,16},{9,1},{1... | collective-permute-start | bytes 1474568 | tf_op jit(solution)/shard_map/ppermute | solution.py:204
  52.4 10.4 %collective-permute-start.13 = (bf16[384,640]{1,0:T(8,128)(2,1)S(1)}, bf16[384,640]{1,0:T(8,128)(2,1)S(1)}, u32[]{:S(2)}, u32[]{:S(2)}) collective-permute-start(bf16[384,640]{1,0:T(8,128)(2,1)S(1)} %add_convert_fusion.5), channel_id=1, source_target_pairs={{0,8},{1,5},{2,10},{3,7},{4,0},{5,13},{6,2},{7,15},{8,16},{9,1},{1... | collective-permute-start | bytes 1474568 | tf_op jit(solution)/shard_map/ppermute | solution.py:207
  54.2 12.3 %collective-permute-start.7 = (bf16[640,384]{1,0:T(8,128)(2,1)S(1)}, bf16[640,384]{1,0:T(8,128)(2,1)S(1)}, u32[]{:S(2)}, u32[]{:S(2)}) collective-permute-start(bf16[640,384]{1,0:T(8,128)(2,1)S(1)} %collective-permute-done.6.far_ref), channel_id=1, source_target_pairs={{0,8},{1,5},{2,10},{3,7},{4,0},{5,13},{6,2},{7,15},{8,16},{9,1},{1... | collective-permute-start | bytes 1474568 | tf_op jit(solution)/shard_map/ppermute | solution.py:204
  62.9 12.2 %collective-permute-start.14 = (bf16[384,640]{1,0:T(8,128)(2,1)S(1)}, bf16[384,640]{1,0:T(8,128)(2,1)S(1)}, u32[]{:S(2)}, u32[]{:S(2)}) collective-permute-start(bf16[384,640]{1,0:T(8,128)(2,1)S(1)} %add_convert_fusion.4), channel_id=1, source_target_pairs={{0,8},{1,5},{2,10},{3,7},{4,0},{5,13},{6,2},{7,15},{8,16},{9,1},{1... | collective-permute-start | bytes 1474568 | tf_op jit(solution)/shard_map/ppermute | solution.py:207
  66.6 10.5 %collective-permute-start.8 = (bf16[640,384]{1,0:T(8,128)(2,1)S(1)}, bf16[640,384]{1,0:T(8,128)(2,1)S(1)}, u32[]{:S(2)}, u32[]{:S(2)}) collective-permute-start(bf16[640,384]{1,0:T(8,128)(2,1)S(1)} %collective-permute-done.7.far_ref), channel_id=1, source_target_pairs={{0,8},{1,5},{2,10},{3,7},{4,0},{5,13},{6,2},{7,15},{8,16},{9,1},{1... | collective-permute-start | bytes 1474568 | tf_op jit(solution)/shard_map/ppermute | solution.py:204
  75.3 10.4 %collective-permute-start.15 = (bf16[384,640]{1,0:T(8,128)(2,1)S(1)}, bf16[384,640]{1,0:T(8,128)(2,1)S(1)}, u32[]{:S(2)}, u32[]{:S(2)}) collective-permute-start(bf16[384,640]{1,0:T(8,128)(2,1)S(1)} %add_convert_fusion.3), channel_id=1, source_target_pairs={{0,8},{1,5},{2,10},{3,7},{4,0},{5,13},{6,2},{7,15},{8,16},{9,1},{1... | collective-permute-start | bytes 1474568 | tf_op jit(solution)/shard_map/ppermute | solution.py:207
  77.1 12.3 %collective-permute-start.9 = (bf16[640,384]{1,0:T(8,128)(2,1)S(1)}, bf16[640,384]{1,0:T(8,128)(2,1)S(1)}, u32[]{:S(2)}, u32[]{:S(2)}) collective-permute-start(bf16[640,384]{1,0:T(8,128)(2,1)S(1)} %collective-permute-done.8.far_ref), channel_id=1, source_target_pairs={{0,8},{1,5},{2,10},{3,7},{4,0},{5,13},{6,2},{7,15},{8,16},{9,1},{1... | collective-permute-start | bytes 1474568 | tf_op jit(solution)/shard_map/ppermute | solution.py:204
  85.8 12.2 %collective-permute-start.16 = (bf16[384,640]{1,0:T(8,128)(2,1)S(1)}, bf16[384,640]{1,0:T(8,128)(2,1)S(1)}, u32[]{:S(2)}, u32[]{:S(2)}) collective-permute-start(bf16[384,640]{1,0:T(8,128)(2,1)S(1)} %add_convert_fusion.2), channel_id=1, source_target_pairs={{0,8},{1,5},{2,10},{3,7},{4,0},{5,13},{6,2},{7,15},{8,16},{9,1},{1... | collective-permute-start | bytes 1474568 | tf_op jit(solution)/shard_map/ppermute | solution.py:207
  89.4 10.5 %collective-permute-start.10 = (bf16[640,384]{1,0:T(8,128)(2,1)S(1)}, bf16[640,384]{1,0:T(8,128)(2,1)S(1)}, u32[]{:S(2)}, u32[]{:S(2)}) collective-permute-start(bf16[640,384]{1,0:T(8,128)(2,1)S(1)} %collective-permute-done.9.far_ref), channel_id=1, source_target_pairs={{0,8},{1,5},{2,10},{3,7},{4,0},{5,13},{6,2},{7,15},{8,16},{9,1},{1... | collective-permute-start | bytes 1474568 | tf_op jit(solution)/shard_map/ppermute | solution.py:204
  98.1 8.9 %collective-permute-start.17 = (bf16[384,640]{1,0:T(8,128)(2,1)S(1)}, bf16[384,640]{1,0:T(8,128)(2,1)S(1)}, u32[]{:S(2)}, u32[]{:S(2)}) collective-permute-start(bf16[384,640]{1,0:T(8,128)(2,1)S(1)} %add_convert_fusion.1), channel_id=1, source_target_pairs={{0,8},{1,5},{2,10},{3,7},{4,0},{5,13},{6,2},{7,15},{8,16},{9,1},{1... | collective-permute-start | bytes 1474568 | tf_op jit(solution)/shard_map/ppermute | solution.py:207
  107.1 6.2 %collective-permute-start.18 = (bf16[192,640]{1,0:T(8,128)(2,1)S(1)}, bf16[192,640]{1,0:T(8,128)(2,1)S(1)}, u32[]{:S(2)}, u32[]{:S(2)}) collective-permute-start(bf16[192,640]{1,0:T(8,128)(2,1)S(1)} %get-tuple-element.66.upper_ref), channel_id=1, source_target_pairs={{0,8},{1,5},{2,10},{3,7},{4,0},{5,13},{6,2},{7,15},{8,16},{9,1},{1... | collective-permute-start | bytes 737288 | tf_op jit(solution)/shard_map/ppermute | solution.py:217
  108.7 7.3 %collective-permute-start.20 = (bf16[192,640]{1,0:T(8,128)(2,1)S(1)}, bf16[192,640]{1,0:T(8,128)(2,1)S(1)}, u32[]{:S(2)}, u32[]{:S(2)}) collective-permute-start(bf16[192,640]{1,0:T(8,128)(2,1)S(1)} %get-tuple-element.65.lower_ref), channel_id=1, source_target_pairs={{0,8},{1,5},{2,10},{3,7},{4,0},{5,13},{6,2},{7,15},{8,16},{9,1},{1... | collective-permute-start | bytes 737288 | tf_op jit(solution)/shard_map/ppermute | solution.py:217
  113.4 6.2 %collective-permute-start.19 = (bf16[192,640]{1,0:T(8,128)(2,1)S(1)}, bf16[192,640]{1,0:T(8,128)(2,1)S(1)}, u32[]{:S(2)}, u32[]{:S(2)}) collective-permute-start(bf16[192,640]{1,0:T(8,128)(2,1)S(1)} %collective-permute-done.18.upper_ref), channel_id=1, source_target_pairs={{0,8},{1,5},{2,10},{3,7},{4,0},{5,13},{6,2},{7,15},{8,16},{9,1},{1... | collective-permute-start | bytes 737288 | tf_op jit(solution)/shard_map/ppermute | solution.py:217
  116.0 6.2 %collective-permute-start.22 = (bf16[192,640]{1,0:T(8,128)(2,1)S(1)}, bf16[192,640]{1,0:T(8,128)(2,1)S(1)}, u32[]{:S(2)}, u32[]{:S(2)}) collective-permute-start(bf16[192,640]{1,0:T(8,128)(2,1)S(1)} %collective-permute-done.20.lower_ref), channel_id=1, source_target_pairs={{0,8},{1,5},{2,10},{3,7},{4,0},{5,13},{6,2},{7,15},{8,16},{9,1},{1... | collective-permute-start | bytes 737288 | tf_op jit(solution)/shard_map/ppermute | solution.py:217
  119.6 6.2 %collective-permute-start.21 = (bf16[192,640]{1,0:T(8,128)(2,1)S(1)}, bf16[192,640]{1,0:T(8,128)(2,1)S(1)}, u32[]{:S(2)}, u32[]{:S(2)}) collective-permute-start(bf16[192,640]{1,0:T(8,128)(2,1)S(1)} %collective-permute-done.19.upper_ref), channel_id=1, source_target_pairs={{0,8},{1,5},{2,10},{3,7},{4,0},{5,13},{6,2},{7,15},{8,16},{9,1},{1... | collective-permute-start | bytes 737288 | tf_op jit(solution)/shard_map/ppermute | solution.py:217
  122.2 6.3 %collective-permute-start.24 = (bf16[192,640]{1,0:T(8,128)(2,1)S(1)}, bf16[192,640]{1,0:T(8,128)(2,1)S(1)}, u32[]{:S(2)}, u32[]{:S(2)}) collective-permute-start(bf16[192,640]{1,0:T(8,128)(2,1)S(1)} %collective-permute-done.22.lower_ref), channel_id=1, source_target_pairs={{0,8},{1,5},{2,10},{3,7},{4,0},{5,13},{6,2},{7,15},{8,16},{9,1},{1... | collective-permute-start | bytes 737288 | tf_op jit(solution)/shard_map/ppermute | solution.py:217
  125.9 6.2 %collective-permute-start.23 = (bf16[192,640]{1,0:T(8,128)(2,1)S(1)}, bf16[192,640]{1,0:T(8,128)(2,1)S(1)}, u32[]{:S(2)}, u32[]{:S(2)}) collective-permute-start(bf16[192,640]{1,0:T(8,128)(2,1)S(1)} %collective-permute-done.21.upper_ref), channel_id=1, source_target_pairs={{0,8},{1,5},{2,10},{3,7},{4,0},{5,13},{6,2},{7,15},{8,16},{9,1},{1... | collective-permute-start | bytes 737288 | tf_op jit(solution)/shard_map/ppermute | solution.py:217
  128.5 6.2 %collective-permute-start.26 = (bf16[192,640]{1,0:T(8,128)(2,1)S(1)}, bf16[192,640]{1,0:T(8,128)(2,1)S(1)}, u32[]{:S(2)}, u32[]{:S(2)}) collective-permute-start(bf16[192,640]{1,0:T(8,128)(2,1)S(1)} %collective-permute-done.24.lower_ref), channel_id=1, source_target_pairs={{0,8},{1,5},{2,10},{3,7},{4,0},{5,13},{6,2},{7,15},{8,16},{9,1},{1... | collective-permute-start | bytes 737288 | tf_op jit(solution)/shard_map/ppermute | solution.py:217
  132.1 6.2 %collective-permute-start.25 = (bf16[192,640]{1,0:T(8,128)(2,1)S(1)}, bf16[192,640]{1,0:T(8,128)(2,1)S(1)}, u32[]{:S(2)}, u32[]{:S(2)}) collective-permute-start(bf16[192,640]{1,0:T(8,128)(2,1)S(1)} %collective-permute-done.23.upper_ref), channel_id=1, source_target_pairs={{0,8},{1,5},{2,10},{3,7},{4,0},{5,13},{6,2},{7,15},{8,16},{9,1},{1... | collective-permute-start | bytes 737288 | tf_op jit(solution)/shard_map/ppermute | solution.py:217
  134.7 6.2 %collective-permute-start.28 = (bf16[192,640]{1,0:T(8,128)(2,1)S(1)}, bf16[192,640]{1,0:T(8,128)(2,1)S(1)}, u32[]{:S(2)}, u32[]{:S(2)}) collective-permute-start(bf16[192,640]{1,0:T(8,128)(2,1)S(1)} %collective-permute-done.26.lower_ref), channel_id=1, source_target_pairs={{0,8},{1,5},{2,10},{3,7},{4,0},{5,13},{6,2},{7,15},{8,16},{9,1},{1... | collective-permute-start | bytes 737288 | tf_op jit(solution)/shard_map/ppermute | solution.py:217
  138.3 6.2 %collective-permute-start.27 = (bf16[192,640]{1,0:T(8,128)(2,1)S(1)}, bf16[192,640]{1,0:T(8,128)(2,1)S(1)}, u32[]{:S(2)}, u32[]{:S(2)}) collective-permute-start(bf16[192,640]{1,0:T(8,128)(2,1)S(1)} %collective-permute-done.25.upper_ref), channel_id=1, source_target_pairs={{0,8},{1,5},{2,10},{3,7},{4,0},{5,13},{6,2},{7,15},{8,16},{9,1},{1... | collective-permute-start | bytes 737288 | tf_op jit(solution)/shard_map/ppermute | solution.py:217
  140.9 6.2 %collective-permute-start.30 = (bf16[192,640]{1,0:T(8,128)(2,1)S(1)}, bf16[192,640]{1,0:T(8,128)(2,1)S(1)}, u32[]{:S(2)}, u32[]{:S(2)}) collective-permute-start(bf16[192,640]{1,0:T(8,128)(2,1)S(1)} %collective-permute-done.28.lower_ref), channel_id=1, source_target_pairs={{0,8},{1,5},{2,10},{3,7},{4,0},{5,13},{6,2},{7,15},{8,16},{9,1},{1... | collective-permute-start | bytes 737288 | tf_op jit(solution)/shard_map/ppermute | solution.py:217
  144.5 6.2 %collective-permute-start.29 = (bf16[192,640]{1,0:T(8,128)(2,1)S(1)}, bf16[192,640]{1,0:T(8,128)(2,1)S(1)}, u32[]{:S(2)}, u32[]{:S(2)}) collective-permute-start(bf16[192,640]{1,0:T(8,128)(2,1)S(1)} %collective-permute-done.27.upper_ref), channel_id=1, source_target_pairs={{0,8},{1,5},{2,10},{3,7},{4,0},{5,13},{6,2},{7,15},{8,16},{9,1},{1... | collective-permute-start | bytes 737288 | tf_op jit(solution)/shard_map/ppermute | solution.py:217
  147.1 6.2 %collective-permute-start.31 = (bf16[192,640]{1,0:T(8,128)(2,1)S(1)}, bf16[192,640]{1,0:T(8,128)(2,1)S(1)}, u32[]{:S(2)}, u32[]{:S(2)}) collective-permute-start(bf16[192,640]{1,0:T(8,128)(2,1)S(1)} %collective-permute-done.30.lower_ref), channel_id=1, source_target_pairs={{0,8},{1,5},{2,10},{3,7},{4,0},{5,13},{6,2},{7,15},{8,16},{9,1},{1... | collective-permute-start | bytes 737288 | tf_op jit(solution)/shard_map/ppermute | solution.py:217
  156.0 4.9 %collective-permute-start.33 = (bf16[1,128,384]{2,1,0:T(8,128)(2,1)S(1)}, bf16[1,128,384]{2,1,0:T(8,128)(2,1)S(1)}, u32[]{:S(2)}, u32[]{:S(2)}) collective-permute-start(bf16[1,128,384]{2,1,0:T(8,128)(2,1)S(1)} %dynamic-slice_convert_fusion), channel_id=1, source_target_pairs={{0,2},{1,3},{2,0},{3,1},{4,6},{5,7},{6,4},{7,5},{8,10},{9,11},{10,... | collective-permute-start | bytes 294920 | tf_op jit(solution)/shard_map/ppermute | solution.py:227
  (2 other events, 4.0 us)
where the time goes:
time: 162 us
  Pallas kernels  72.1 us (45%)
  starting transfers between devices  50 us (31%)
  waiting for transfers between devices  36.9 us (23%)
    pallas_call x7, Pallas kernels, partial_of(): pl.pallas_call(next_kernel, out_shape=sums, grid_spec=pltpu.PrefetchScala...  49.1 us
    ppermute x14, starting transfers between devices, local(): after = (lax.ppermute(upper, AXES, hop), lax.ppermute(lower, AXES, hop))  20.2 us
    pallas_call x8, Pallas kernels, term_of(): pl.pallas_call(functools.partial(term_kernel, k, rows), out_shape=(sums,)...  15.7 us
    ppermute x3, waiting for transfers between devices, local(): held.append((mask ^ bit, lax.ppermute(block, AXES, swap(bit))))  12 us
    ppermute x14, waiting for transfers between devices, local(): after = (lax.ppermute(upper, AXES, hop), lax.ppermute(lower, AXES, hop))  11.3 us
    ppermute x7, starting transfers between devices, local(): following = lax.ppermute(far, AXES, hop) if k < rows - 1 else None  11.2 us
    ppermute x7, starting transfers between devices, local(): part = part + lax.ppermute(sent, AXES, hop).astype(jnp.float32)  10.8 us
    ppermute x7, waiting for transfers between devices, local(): following = lax.ppermute(far, AXES, hop) if k < rows - 1 else None  7.36 us
  transfers between devices with their start and end apart: 34, of which 22 were waited for; matrix products, arithmetic and copies ran while one was open for 1% of the time, Pallas kernels for 44%

commit v1 on v0

--- a/solution.py
+++ b/solution.py
@@ -61,13 +61,14 @@
 def first_kernel(count, where, *refs):
     shards, (far_ref, coulomb_ref, out_ref, near_ref) = refs[:count], refs[count:]
     share = shards[0].shape[0]
+    start = where[where.shape[0] - count + pl.program_id(0)] * share
+    rows = pl.ds(pl.multiple_of(start, share), share)
     for q in range(count):
 
         @pl.when(pl.program_id(0) == q)
         def _():
-            near_ref[q * share : (q + 1) * share, :] = shards[q][...]
-
-    rows = pl.ds(pl.multiple_of(pl.program_id(0) * share, share), share)
+            near_ref[rows, :] = shards[q][...]
+
     accumulate(near_ref[rows, :], far_ref, coulomb_ref, out_ref)
 
 
@@ -93,10 +94,10 @@
     sums = jax.ShapeDtypeStruct((norb, share), jnp.float32)
     sums_spec = pl.BlockSpec((norb, share), fixed)
     shard_spec = pl.BlockSpec((share, norb), fixed)
-    tail_specs = [shard_spec, pl.BlockSpec((share, share), lambda i, w: (w[rows + i], w[k]))]
     m = count * share
+    tile = 2 * share if count % 2 == 0 else share
     options = dict(
-        compiler_params=pltpu.CompilerParams(vmem_limit_bytes=20 << 20),
+        compiler_params=pltpu.CompilerParams(vmem_limit_bytes=24 << 20),
         cost_estimate=pl.CostEstimate(
             flops=4 * m * norb * share, bytes_accessed=4 * m * share, transcendentals=0
         ),
@@ -109,7 +110,8 @@
             grid_spec=pltpu.PrefetchScalarGridSpec(
                 num_scalar_prefetch=1,
                 grid=(count,),
-                in_specs=[shard_spec] * count + tail_specs,
+                in_specs=[shard_spec] * (count + 1)
+                + [pl.BlockSpec((share, share), lambda i, w: (w[rows + i], w[k]))],
                 out_specs=(sums_spec, pl.BlockSpec((m, norb), fixed)),
             ),
             **options,
@@ -119,8 +121,12 @@
         out_shape=sums,
         grid_spec=pltpu.PrefetchScalarGridSpec(
             num_scalar_prefetch=1,
-            grid=(count,),
-            in_specs=[pl.BlockSpec((share, norb), lambda i, w: (i, 0))] + tail_specs,
+            grid=(m // tile,),
+            in_specs=[
+                pl.BlockSpec((tile, norb), lambda i, w: (i, 0)),
+                shard_spec,
+                pl.BlockSpec((tile, share), lambda i, w: (i, w[k])),
+            ],
             out_specs=sums_spec,
         ),
         **options,
@@ -187,10 +193,11 @@
     deal, hop, swap, table = plan(rows, cols)
     _, norb = orbitals.shape
     row, col = lax.axis_index("row"), lax.axis_index("col")
+    far = lax.ppermute(orbitals, AXES, deal)
+    far, landed = lax.optimization_barrier((far, row))
     table = jnp.asarray(table, jnp.int32)
-    where = lax.dynamic_slice(table, (row, col, 0), (1, 1, rows + cols)).reshape(rows + cols)
-
-    far = lax.ppermute(orbitals, AXES, deal)
+    where = lax.dynamic_slice(table, (landed, col, 0), (1, 1, rows + cols)).reshape(-1)
+
     held = [(0, orbitals)]
     bit = cols // 2
     while bit:
@@ -211,12 +218,11 @@
     cut = norb // 32 * 16
     upper, lower, total, block = sent[:cut], sent[cut:], None, None
     for k in range(rows):
-        if total is not None:
-            upper, total = lax.optimization_barrier((upper, total))
         if k < rows - 1:
-            after = lax.ppermute(upper, AXES, hop), lax.ppermute(lower, AXES, hop)
+            upper_next = lax.ppermute(upper, AXES, hop)
+            lower_next = lax.ppermute(lower, AXES, hop)
         total, block = term_of(k, rows, where, interp, upper, lower, total, block)
-        upper, lower = after
+        upper, lower = upper_next, lower_next
 
     bit, blocks = 1, cols
     while bit < cols:

time: 162 us -> 171 us (1.056)
  waiting for transfers between devices: 36.9 us -> 47.3 us
  Pallas kernels: 72.1 us -> 69.5 us
    ppermute x14, waiting for transfers between devices: 11.3 us -> 20.3 us  [the longest x7 13.7 us: local(): upper_next = lax.ppermute(upper, AXES, hop)]
    pallas_call x7, Pallas kernels: 49.1 us -> 45.9 us  [partial_of(): pl.pallas_call(next_kernel, out_shape=sums, grid_spec=pltpu.PrefetchScala...]
    ppermute x7, waiting for transfers between devices: 7.36 us -> 9.16 us  [local(): following = lax.ppermute(far, AXES, hop) if k < rows - 1 else None]
  transfers between devices with their start and end apart: 34 -> 34, of which waited for: 22 -> 21; matrix products, arithmetic and copies ran while one was open for 1% -> 1% of each run, Pallas kernels for 44% -> 40%
where the time goes in v1:
time: 171 us
  Pallas kernels  69.5 us (41%)
  starting transfers between devices  51.3 us (30%)
  waiting for transfers between devices  47.3 us (28%)
    pallas_call x7, Pallas kernels, partial_of(): pl.pallas_call(next_kernel, out_shape=sums, grid_spec=pltpu.PrefetchScala...  45.9 us
    pallas_call x8, Pallas kernels, term_of(): pl.pallas_call(functools.partial(term_kernel, k, rows), out_shape=(sums,)...  16.3 us
    ppermute x7, waiting for transfers between devices, local(): upper_next = lax.ppermute(upper, AXES, hop)  13.7 us
    ppermute x3, waiting for transfers between devices, local(): held.append((mask ^ bit, lax.ppermute(block, AXES, swap(bit))))  12 us
    ppermute x7, starting transfers between devices, local(): following = lax.ppermute(far, AXES, hop) if k < rows - 1 else None  11.2 us
    ppermute x7, starting transfers between devices, local(): part = part + lax.ppermute(sent, AXES, hop).astype(jnp.float32)  10.8 us
    ppermute x7, starting transfers between devices, local(): upper_next = lax.ppermute(upper, AXES, hop)  10.8 us
    ppermute x7, starting transfers between devices, local(): lower_next = lax.ppermute(lower, AXES, hop)  10.3 us
  transfers between devices with their start and end apart: 34, of which 21 were waited for; matrix products, arithmetic and copies ran while one was open for 1% of the time, Pallas kernels for 40%

profile of v1, /device:TPU:0, one launch (start us, length us, event | category | flops | bytes accessed | tf_op | source)
XLA Modules:
  0.0 170.8 jit_solution(13015942310393669311)
XLA Ops:
  0.0 3.0 %collective-permute-start.2 = (bf16[640,384]{1,0:T(8,128)(2,1)}, bf16[640,384]{1,0:T(8,128)(2,1)S(1)}, u32[]{:S(2)}, u32[]{:S(2)}) collective-permute-start(bf16[640,384]{1,0:T(8,128)(2,1)} %refs_0_.1), channel_id=1, source_target_pairs={{0,2},{1,3},{2,0},{3,1},{4,6},{5,7},{6,4},{7,5},{8,10},{9,11},{10,... | collective-permute-start | bytes 1474568 | tf_op jit(solution)/shard_map/ppermute | solution.py:205
  3.0 1.7 collective-permute-start
  4.6 3.0 %collective-permute-start.1 = (bf16[640,384]{1,0:T(8,128)(2,1)}, bf16[640,384]{1,0:T(8,128)(2,1)S(1)}, u32[]{:S(2)}, u32[]{:S(2)}) collective-permute-start(bf16[640,384]{1,0:T(8,128)(2,1)} %refs_0_.1), channel_id=1, source_target_pairs={{0,1},{1,0},{2,3},{3,2},{4,5},{5,4},{6,7},{7,6},{8,9},{9,8},{10,11... | collective-permute-start | bytes 1474568 | tf_op jit(solution)/shard_map/ppermute | solution.py:205
  7.6 12.0 %collective-permute-done.2.refs_2_ = bf16[640,384]{1,0:T(8,128)(2,1)S(1)} collective-permute-done((bf16[640,384]{1,0:T(8,128)(2,1)}, bf16[640,384]{1,0:T(8,128)(2,1)S(1)}, u32[]{:S(2)}, u32[]{:S(2)}) %collective-permute-start.2) | collective-permute-done | bytes 491552 | tf_op jit(solution)/shard_map/ppermute | solution.py:205
  19.7 1.8 %collective-permute-start.4 = (bf16[640,384]{1,0:T(8,128)(2,1)S(1)}, bf16[640,384]{1,0:T(8,128)(2,1)S(1)}, u32[]{:S(2)}, u32[]{:S(2)}) collective-permute-start(bf16[640,384]{1,0:T(8,128)(2,1)S(1)} %collective-permute-done.refs_4_), channel_id=1, source_target_pairs={{0,8},{1,5},{2,10},{3,7},{4,0},{5,13},{6,2},{7,15},{8,16},{9,1},{1... | collective-permute-start | bytes 1474568 | tf_op jit(solution)/shard_map/ppermute | solution.py:211
  22.2 7.3 %partial.8 = (f32[384,640]{1,0:T(8,128)S(1)}, bf16[2560,384]{1,0:T(8,128)(2,1)S(1)}) custom-call(s32[12]{0:T(128)S(1)} %fusion.2.where, bf16[640,384]{1,0:T(8,128)(2,1)} %refs_0_.1, bf16[640,384]{1,0:T(8,128)(2,1)S(1)} %collective-permute-done.1.refs_1_, bf16[640,384]{1,0:T(8,128)(2,1)S(1)} %collective-permute-done.2.refs_2_, ...), custom_call_target="tpu_custom_call" | custom-call | flops 2516582400 | bytes 6553600 | tf_op jit(solution)/shard_map/partial/pallas_call | solution.py:107
  29.6 1.6 collective-permute-start.11
  32.8 6.5 %partial.15 = f32[384,640]{1,0:T(8,128)S(1)} custom-call(s32[12]{0:T(128)S(1)} %fusion.2.where, bf16[2560,384]{1,0:T(8,128)(2,1)S(1)} %get-tuple-element.25.near_ref, bf16[640,384]{1,0:T(8,128)(2,1)S(1)} %collective-permute-done.4.far_ref, f32[2560,5120]{1,0:T(8,128)} %coulomb_ref.13), custom_call_target="tpu_custom_call" | custom-call | flops 2516582400 | bytes 6553600 | tf_op jit(solution)/shard_map/partial/pallas_call | solution.py:119
  41.0 2.7 %collective-permute-done.5.far_ref = bf16[640,384]{1,0:T(8,128)(2,1)S(1)} collective-permute-done((bf16[640,384]{1,0:T(8,128)(2,1)S(1)}, bf16[640,384]{1,0:T(8,128)(2,1)S(1)}, u32[]{:S(2)}, u32[]{:S(2)}) %collective-permute-start.5) | collective-permute-done | bytes 491552 | tf_op jit(solution)/shard_map/ppermute | solution.py:211
  45.3 6.6 %partial.14 = f32[384,640]{1,0:T(8,128)S(1)} custom-call(s32[12]{0:T(128)S(1)} %fusion.2.where, bf16[2560,384]{1,0:T(8,128)(2,1)S(1)} %get-tuple-element.25.near_ref, bf16[640,384]{1,0:T(8,128)(2,1)S(1)} %collective-permute-done.5.far_ref, f32[2560,5120]{1,0:T(8,128)} %coulomb_ref.13), custom_call_target="tpu_custom_call" | custom-call | flops 2516582400 | bytes 6553600 | tf_op jit(solution)/shard_map/partial/pallas_call | solution.py:119
  55.8 6.6 %partial.13 = f32[384,640]{1,0:T(8,128)S(1)} custom-call(s32[12]{0:T(128)S(1)} %fusion.2.where, bf16[2560,384]{1,0:T(8,128)(2,1)S(1)} %get-tuple-element.25.near_ref, bf16[640,384]{1,0:T(8,128)(2,1)S(1)} %collective-permute-done.6.far_ref, f32[2560,5120]{1,0:T(8,128)} %coulomb_ref.13), custom_call_target="tpu_custom_call" | custom-call | flops 2516582400 | bytes 6553600 | tf_op jit(solution)/shard_map/partial/pallas_call | solution.py:119
  64.1 2.0 %collective-permute-done.7.far_ref = bf16[640,384]{1,0:T(8,128)(2,1)S(1)} collective-permute-done((bf16[640,384]{1,0:T(8,128)(2,1)S(1)}, bf16[640,384]{1,0:T(8,128)(2,1)S(1)}, u32[]{:S(2)}, u32[]{:S(2)}) %collective-permute-start.7) | collective-permute-done | bytes 491552 | tf_op jit(solution)/shard_map/ppermute | solution.py:211
  67.7 6.6 %partial.12 = f32[384,640]{1,0:T(8,128)S(1)} custom-call(s32[12]{0:T(128)S(1)} %fusion.2.where, bf16[2560,384]{1,0:T(8,128)(2,1)S(1)} %get-tuple-element.25.near_ref, bf16[640,384]{1,0:T(8,128)(2,1)S(1)} %collective-permute-done.7.far_ref, f32[2560,5120]{1,0:T(8,128)} %coulomb_ref.13), custom_call_target="tpu_custom_call" | custom-call | flops 2516582400 | bytes 6553600 | tf_op jit(solution)/shard_map/partial/pallas_call | solution.py:119
  78.3 6.6 %partial.11 = f32[384,640]{1,0:T(8,128)S(1)} custom-call(s32[12]{0:T(128)S(1)} %fusion.2.where, bf16[2560,384]{1,0:T(8,128)(2,1)S(1)} %get-tuple-element.25.near_ref, bf16[640,384]{1,0:T(8,128)(2,1)S(1)} %collective-permute-done.8.far_ref, f32[2560,5120]{1,0:T(8,128)} %coulomb_ref.13), custom_call_target="tpu_custom_call" | custom-call | flops 2516582400 | bytes 6553600 | tf_op jit(solution)/shard_map/partial/pallas_call | solution.py:119
  86.5 2.0 %collective-permute-done.9.far_ref = bf16[640,384]{1,0:T(8,128)(2,1)S(1)} collective-permute-done((bf16[640,384]{1,0:T(8,128)(2,1)S(1)}, bf16[640,384]{1,0:T(8,128)(2,1)S(1)}, u32[]{:S(2)}, u32[]{:S(2)}) %collective-permute-start.9) | collective-permute-done | bytes 491552 | tf_op jit(solution)/shard_map/ppermute | solution.py:211
  90.1 6.6 %partial.10 = f32[384,640]{1,0:T(8,128)S(1)} custom-call(s32[12]{0:T(128)S(1)} %fusion.2.where, bf16[2560,384]{1,0:T(8,128)(2,1)S(1)} %get-tuple-element.25.near_ref, bf16[640,384]{1,0:T(8,128)(2,1)S(1)} %collective-permute-done.9.far_ref, f32[2560,5120]{1,0:T(8,128)} %coulomb_ref.13), custom_call_target="tpu_custom_call" | custom-call | flops 2516582400 | bytes 6553600 | tf_op jit(solution)/shard_map/partial/pallas_call | solution.py:119
  99.1 6.6 %partial.9 = f32[384,640]{1,0:T(8,128)S(1)} custom-call(s32[12]{0:T(128)S(1)} %fusion.2.where, bf16[2560,384]{1,0:T(8,128)(2,1)S(1)} %get-tuple-element.25.near_ref, bf16[640,384]{1,0:T(8,128)(2,1)S(1)} %collective-permute-done.10.far_ref, f32[2560,5120]{1,0:T(8,128)} %coulomb_ref.13), custom_call_target="tpu_custom_call" | custom-call | flops 2516582400 | bytes 6553600 | tf_op jit(solution)/shard_map/partial/pallas_call | solution.py:119
  108.6 3.5 %collective-permute-done.18.upper_ref = bf16[192,640]{1,0:T(8,128)(2,1)S(1)} collective-permute-done((bf16[192,640]{1,0:T(8,128)(2,1)S(1)}, bf16[192,640]{1,0:T(8,128)(2,1)S(1)}, u32[]{:S(2)}, u32[]{:S(2)}) %collective-permute-start.18) | collective-permute-done | bytes 245792 | tf_op jit(solution)/shard_map/ppermute | solution.py:222
  116.2 2.0 %collective-permute-done.19.upper_ref = bf16[192,640]{1,0:T(8,128)(2,1)S(1)} collective-permute-done((bf16[192,640]{1,0:T(8,128)(2,1)S(1)}, bf16[192,640]{1,0:T(8,128)(2,1)S(1)}, u32[]{:S(2)}, u32[]{:S(2)}) %collective-permute-start.19) | collective-permute-done | bytes 245792 | tf_op jit(solution)/shard_map/ppermute | solution.py:222
  122.4 2.0 %collective-permute-done.20.upper_ref = bf16[192,640]{1,0:T(8,128)(2,1)S(1)} collective-permute-done((bf16[192,640]{1,0:T(8,128)(2,1)S(1)}, bf16[192,640]{1,0:T(8,128)(2,1)S(1)}, u32[]{:S(2)}, u32[]{:S(2)}) %collective-permute-start.20) | collective-permute-done | bytes 245792 | tf_op jit(solution)/shard_map/ppermute | solution.py:222
  128.6 2.0 %collective-permute-done.21.upper_ref = bf16[192,640]{1,0:T(8,128)(2,1)S(1)} collective-permute-done((bf16[192,640]{1,0:T(8,128)(2,1)S(1)}, bf16[192,640]{1,0:T(8,128)(2,1)S(1)}, u32[]{:S(2)}, u32[]{:S(2)}) %collective-permute-start.21) | collective-permute-done | bytes 245792 | tf_op jit(solution)/shard_map/ppermute | solution.py:222
  134.8 2.0 %collective-permute-done.22.upper_ref = bf16[192,640]{1,0:T(8,128)(2,1)S(1)} collective-permute-done((bf16[192,640]{1,0:T(8,128)(2,1)S(1)}, bf16[192,640]{1,0:T(8,128)(2,1)S(1)}, u32[]{:S(2)}, u32[]{:S(2)}) %collective-permute-start.22) | collective-permute-done | bytes 245792 | tf_op jit(solution)/shard_map/ppermute | solution.py:222
  141.0 2.0 %collective-permute-done.23.upper_ref = bf16[192,640]{1,0:T(8,128)(2,1)S(1)} collective-permute-done((bf16[192,640]{1,0:T(8,128)(2,1)S(1)}, bf16[192,640]{1,0:T(8,128)(2,1)S(1)}, u32[]{:S(2)}, u32[]{:S(2)}) %collective-permute-start.23) | collective-permute-done | bytes 245792 | tf_op jit(solution)/shard_map/ppermute | solution.py:222
  147.2 2.2 %term.8 = (f32[512,384]{1,0:T(8,128)S(1)}, bf16[512,640]{1,0:T(8,128)(2,1)S(1)}) custom-call(s32[12]{0:T(128)S(1)} %fusion.2.where, bf16[512,5120]{1,0:T(8,128)(2,1)} %interp_ref.15, bf16[192,640]{1,0:T(8,128)(2,1)S(1)} %get-tuple-element.42.upper_ref, bf16[192,640]{1,0:T(8,128)(2,1)S(1)} %get-tuple-element.41.lower_ref), custom_call_target="tpu_custom_call" | custom-call | flops 251658240 | bytes 655360 | tf_op jit(solution)/shard_map/term/pallas_call | solution.py:175
  149.4 2.1 %term.9 = (f32[512,384]{1,0:T(8,128)S(1)}, bf16[512,640]{1,0:T(8,128)(2,1)S(1)}) custom-call(s32[12]{0:T(128)S(1)} %fusion.2.where, bf16[512,5120]{1,0:T(8,128)(2,1)} %interp_ref.15, bf16[192,640]{1,0:T(8,128)(2,1)S(1)} %collective-permute-done.18.upper_ref, bf16[192,640]{1,0:T(8,128)(2,1)S(1)} %collective-permute-done.25.lower_ref, ...), custom_call_target="tpu_custom_call" | custom-call | flops 251658240 | bytes 655360 | tf_op jit(solution)/shard_map/term/pallas_call | solution.py:175
  151.5 2.1 %term.10 = (f32[512,384]{1,0:T(8,128)S(1)}, bf16[512,640]{1,0:T(8,128)(2,1)S(1)}) custom-call(s32[12]{0:T(128)S(1)} %fusion.2.where, bf16[512,5120]{1,0:T(8,128)(2,1)} %interp_ref.15, bf16[192,640]{1,0:T(8,128)(2,1)S(1)} %collective-permute-done.19.upper_ref, bf16[192,640]{1,0:T(8,128)(2,1)S(1)} %collective-permute-done.26.lower_ref, ...), custom_call_target="tpu_custom_call" | custom-call | flops 251658240 | bytes 655360 | tf_op jit(solution)/shard_map/term/pallas_call | solution.py:175
  153.6 2.1 %term.11 = (f32[512,384]{1,0:T(8,128)S(1)}, bf16[512,640]{1,0:T(8,128)(2,1)S(1)}) custom-call(s32[12]{0:T(128)S(1)} %fusion.2.where, bf16[512,5120]{1,0:T(8,128)(2,1)} %interp_ref.15, bf16[192,640]{1,0:T(8,128)(2,1)S(1)} %collective-permute-done.20.upper_ref, bf16[192,640]{1,0:T(8,128)(2,1)S(1)} %collective-permute-done.27.lower_ref, ...), custom_call_target="tpu_custom_call" | custom-call | flops 251658240 | bytes 655360 | tf_op jit(solution)/shard_map/term/pallas_call | solution.py:175
  155.7 2.1 %term.12 = (f32[512,384]{1,0:T(8,128)S(1)}, bf16[512,640]{1,0:T(8,128)(2,1)S(1)}) custom-call(s32[12]{0:T(128)S(1)} %fusion.2.where, bf16[512,5120]{1,0:T(8,128)(2,1)} %interp_ref.15, bf16[192,640]{1,0:T(8,128)(2,1)S(1)} %collective-permute-done.21.upper_ref, bf16[192,640]{1,0:T(8,128)(2,1)S(1)} %collective-permute-done.28.lower_ref, ...), custom_call_target="tpu_custom_call" | custom-call | flops 251658240 | bytes 655360 | tf_op jit(solution)/shard_map/term/pallas_call | solution.py:175
  157.8 2.1 %term.13 = (f32[512,384]{1,0:T(8,128)S(1)}, bf16[512,640]{1,0:T(8,128)(2,1)S(1)}) custom-call(s32[12]{0:T(128)S(1)} %fusion.2.where, bf16[512,5120]{1,0:T(8,128)(2,1)} %interp_ref.15, bf16[192,640]{1,0:T(8,128)(2,1)S(1)} %collective-permute-done.22.upper_ref, bf16[192,640]{1,0:T(8,128)(2,1)S(1)} %collective-permute-done.29.lower_ref, ...), custom_call_target="tpu_custom_call" | custom-call | flops 251658240 | bytes 655360 | tf_op jit(solution)/shard_map/term/pallas_call | solution.py:175
  159.8 2.1 %term.14 = (f32[512,384]{1,0:T(8,128)S(1)}, bf16[512,640]{1,0:T(8,128)(2,1)S(1)}) custom-call(s32[12]{0:T(128)S(1)} %fusion.2.where, bf16[512,5120]{1,0:T(8,128)(2,1)} %interp_ref.15, bf16[192,640]{1,0:T(8,128)(2,1)S(1)} %collective-permute-done.23.upper_ref, bf16[192,640]{1,0:T(8,128)(2,1)S(1)} %collective-permute-done.30.lower_ref, ...), custom_call_target="tpu_custom_call" | custom-call | flops 251658240 | bytes 655360 | tf_op jit(solution)/shard_map/term/pallas_call | solution.py:175
  161.9 1.6 term.15
  165.7 4.5 %collective-permute-done.33 = bf16[1,128,384]{2,1,0:T(8,128)(2,1)S(1)} collective-permute-done((bf16[1,128,384]{2,1,0:T(8,128)(2,1)S(1)}, bf16[1,128,384]{2,1,0:T(8,128)(2,1)S(1)}, u32[]{:S(2)}, u32[]{:S(2)}) %collective-permute-start.33) | collective-permute-done | bytes 98336 | tf_op jit(solution)/shard_map/ppermute | solution.py:233
  (66 shorter events, 53.0 us)
Async XLA Ops:
  0.0 19.7 %collective-permute-start.2 = (bf16[640,384]{1,0:T(8,128)(2,1)}, bf16[640,384]{1,0:T(8,128)(2,1)S(1)}, u32[]{:S(2)}, u32[]{:S(2)}) collective-permute-start(bf16[640,384]{1,0:T(8,128)(2,1)} %refs_0_.1), channel_id=1, source_target_pairs={{0,2},{1,3},{2,0},{3,1},{4,6},{5,7},{6,4},{7,5},{8,10},{9,11},{10,... | collective-permute-start | bytes 1474568 | tf_op jit(solution)/shard_map/ppermute | solution.py:205
  3.0 16.7 %collective-permute-start = (bf16[640,384]{1,0:T(8,128)(2,1)}, bf16[640,384]{1,0:T(8,128)(2,1)S(1)}, u32[]{:S(2)}, u32[]{:S(2)}) collective-permute-start(bf16[640,384]{1,0:T(8,128)(2,1)} %refs_0_.1), channel_id=1, source_target_pairs={{0,0},{1,16},{2,8},{3,24},{4,4},{5,20},{6,12},{7,28},{8,9},{9,25},... | collective-permute-start | bytes 1474568 | tf_op jit(solution)/shard_map/ppermute | solution.py:196
  4.6 17.5 %collective-permute-start.1 = (bf16[640,384]{1,0:T(8,128)(2,1)}, bf16[640,384]{1,0:T(8,128)(2,1)S(1)}, u32[]{:S(2)}, u32[]{:S(2)}) collective-permute-start(bf16[640,384]{1,0:T(8,128)(2,1)} %refs_0_.1), channel_id=1, source_target_pairs={{0,1},{1,0},{2,3},{3,2},{4,5},{5,4},{6,7},{7,6},{8,9},{9,8},{10,11... | collective-permute-start | bytes 1474568 | tf_op jit(solution)/shard_map/ppermute | solution.py:205
  19.7 11.5 %collective-permute-start.4 = (bf16[640,384]{1,0:T(8,128)(2,1)S(1)}, bf16[640,384]{1,0:T(8,128)(2,1)S(1)}, u32[]{:S(2)}, u32[]{:S(2)}) collective-permute-start(bf16[640,384]{1,0:T(8,128)(2,1)S(1)} %collective-permute-done.refs_4_), channel_id=1, source_target_pairs={{0,8},{1,5},{2,10},{3,7},{4,0},{5,13},{6,2},{7,15},{8,16},{9,1},{1... | collective-permute-start | bytes 1474568 | tf_op jit(solution)/shard_map/ppermute | solution.py:211
  29.6 9.8 %collective-permute-start.11 = (bf16[384,640]{1,0:T(8,128)(2,1)S(1)}, bf16[384,640]{1,0:T(8,128)(2,1)S(1)}, u32[]{:S(2)}, u32[]{:S(2)}) collective-permute-start(bf16[384,640]{1,0:T(8,128)(2,1)S(1)} %convert_element_type.68), channel_id=1, source_target_pairs={{0,8},{1,5},{2,10},{3,7},{4,0},{5,13},{6,2},{7,15},{8,16},{9,1},{1... | collective-permute-start | bytes 1474568 | tf_op jit(solution)/shard_map/ppermute | solution.py:214
  31.2 12.5 %collective-permute-start.5 = (bf16[640,384]{1,0:T(8,128)(2,1)S(1)}, bf16[640,384]{1,0:T(8,128)(2,1)S(1)}, u32[]{:S(2)}, u32[]{:S(2)}) collective-permute-start(bf16[640,384]{1,0:T(8,128)(2,1)S(1)} %collective-permute-done.4.far_ref), channel_id=1, source_target_pairs={{0,8},{1,5},{2,10},{3,7},{4,0},{5,13},{6,2},{7,15},{8,16},{9,1},{1... | collective-permute-start | bytes 1474568 | tf_op jit(solution)/shard_map/ppermute | solution.py:211
  39.5 12.4 %collective-permute-start.12 = (bf16[384,640]{1,0:T(8,128)(2,1)S(1)}, bf16[384,640]{1,0:T(8,128)(2,1)S(1)}, u32[]{:S(2)}, u32[]{:S(2)}) collective-permute-start(bf16[384,640]{1,0:T(8,128)(2,1)S(1)} %add_convert_fusion.6), channel_id=1, source_target_pairs={{0,8},{1,5},{2,10},{3,7},{4,0},{5,13},{6,2},{7,15},{8,16},{9,1},{1... | collective-permute-start | bytes 1474568 | tf_op jit(solution)/shard_map/ppermute | solution.py:214
  43.7 10.5 %collective-permute-start.6 = (bf16[640,384]{1,0:T(8,128)(2,1)S(1)}, bf16[640,384]{1,0:T(8,128)(2,1)S(1)}, u32[]{:S(2)}, u32[]{:S(2)}) collective-permute-start(bf16[640,384]{1,0:T(8,128)(2,1)S(1)} %collective-permute-done.5.far_ref), channel_id=1, source_target_pairs={{0,8},{1,5},{2,10},{3,7},{4,0},{5,13},{6,2},{7,15},{8,16},{9,1},{1... | collective-permute-start | bytes 1474568 | tf_op jit(solution)/shard_map/ppermute | solution.py:211
  52.0 10.4 %collective-permute-start.13 = (bf16[384,640]{1,0:T(8,128)(2,1)S(1)}, bf16[384,640]{1,0:T(8,128)(2,1)S(1)}, u32[]{:S(2)}, u32[]{:S(2)}) collective-permute-start(bf16[384,640]{1,0:T(8,128)(2,1)S(1)} %add_convert_fusion.5), channel_id=1, source_target_pairs={{0,8},{1,5},{2,10},{3,7},{4,0},{5,13},{6,2},{7,15},{8,16},{9,1},{1... | collective-permute-start | bytes 1474568 | tf_op jit(solution)/shard_map/ppermute | solution.py:214
  54.3 11.9 %collective-permute-start.7 = (bf16[640,384]{1,0:T(8,128)(2,1)S(1)}, bf16[640,384]{1,0:T(8,128)(2,1)S(1)}, u32[]{:S(2)}, u32[]{:S(2)}) collective-permute-start(bf16[640,384]{1,0:T(8,128)(2,1)S(1)} %collective-permute-done.6.far_ref), channel_id=1, source_target_pairs={{0,8},{1,5},{2,10},{3,7},{4,0},{5,13},{6,2},{7,15},{8,16},{9,1},{1... | collective-permute-start | bytes 1474568 | tf_op jit(solution)/shard_map/ppermute | solution.py:211
  62.5 11.8 %collective-permute-start.14 = (bf16[384,640]{1,0:T(8,128)(2,1)S(1)}, bf16[384,640]{1,0:T(8,128)(2,1)S(1)}, u32[]{:S(2)}, u32[]{:S(2)}) collective-permute-start(bf16[384,640]{1,0:T(8,128)(2,1)S(1)} %add_convert_fusion.4), channel_id=1, source_target_pairs={{0,8},{1,5},{2,10},{3,7},{4,0},{5,13},{6,2},{7,15},{8,16},{9,1},{1... | collective-permute-start | bytes 1474568 | tf_op jit(solution)/shard_map/ppermute | solution.py:214
  66.2 10.5 %collective-permute-start.8 = (bf16[640,384]{1,0:T(8,128)(2,1)S(1)}, bf16[640,384]{1,0:T(8,128)(2,1)S(1)}, u32[]{:S(2)}, u32[]{:S(2)}) collective-permute-start(bf16[640,384]{1,0:T(8,128)(2,1)S(1)} %collective-permute-done.7.far_ref), channel_id=1, source_target_pairs={{0,8},{1,5},{2,10},{3,7},{4,0},{5,13},{6,2},{7,15},{8,16},{9,1},{1... | collective-permute-start | bytes 1474568 | tf_op jit(solution)/shard_map/ppermute | solution.py:211
  74.4 10.4 %collective-permute-start.15 = (bf16[384,640]{1,0:T(8,128)(2,1)S(1)}, bf16[384,640]{1,0:T(8,128)(2,1)S(1)}, u32[]{:S(2)}, u32[]{:S(2)}) collective-permute-start(bf16[384,640]{1,0:T(8,128)(2,1)S(1)} %add_convert_fusion.3), channel_id=1, source_target_pairs={{0,8},{1,5},{2,10},{3,7},{4,0},{5,13},{6,2},{7,15},{8,16},{9,1},{1... | collective-permute-start | bytes 1474568 | tf_op jit(solution)/shard_map/ppermute | solution.py:214
  76.7 11.9 %collective-permute-start.9 = (bf16[640,384]{1,0:T(8,128)(2,1)S(1)}, bf16[640,384]{1,0:T(8,128)(2,1)S(1)}, u32[]{:S(2)}, u32[]{:S(2)}) collective-permute-start(bf16[640,384]{1,0:T(8,128)(2,1)S(1)} %collective-permute-done.8.far_ref), channel_id=1, source_target_pairs={{0,8},{1,5},{2,10},{3,7},{4,0},{5,13},{6,2},{7,15},{8,16},{9,1},{1... | collective-permute-start | bytes 1474568 | tf_op jit(solution)/shard_map/ppermute | solution.py:211
  84.9 11.7 %collective-permute-start.16 = (bf16[384,640]{1,0:T(8,128)(2,1)S(1)}, bf16[384,640]{1,0:T(8,128)(2,1)S(1)}, u32[]{:S(2)}, u32[]{:S(2)}) collective-permute-start(bf16[384,640]{1,0:T(8,128)(2,1)S(1)} %add_convert_fusion.2), channel_id=1, source_target_pairs={{0,8},{1,5},{2,10},{3,7},{4,0},{5,13},{6,2},{7,15},{8,16},{9,1},{1... | collective-permute-start | bytes 1474568 | tf_op jit(solution)/shard_map/ppermute | solution.py:214
  88.6 10.5 %collective-permute-start.10 = (bf16[640,384]{1,0:T(8,128)(2,1)S(1)}, bf16[640,384]{1,0:T(8,128)(2,1)S(1)}, u32[]{:S(2)}, u32[]{:S(2)}) collective-permute-start(bf16[640,384]{1,0:T(8,128)(2,1)S(1)} %collective-permute-done.9.far_ref), channel_id=1, source_target_pairs={{0,8},{1,5},{2,10},{3,7},{4,0},{5,13},{6,2},{7,15},{8,16},{9,1},{1... | collective-permute-start | bytes 1474568 | tf_op jit(solution)/shard_map/ppermute | solution.py:211
  96.8 8.9 %collective-permute-start.17 = (bf16[384,640]{1,0:T(8,128)(2,1)S(1)}, bf16[384,640]{1,0:T(8,128)(2,1)S(1)}, u32[]{:S(2)}, u32[]{:S(2)}) collective-permute-start(bf16[384,640]{1,0:T(8,128)(2,1)S(1)} %add_convert_fusion.1), channel_id=1, source_target_pairs={{0,8},{1,5},{2,10},{3,7},{4,0},{5,13},{6,2},{7,15},{8,16},{9,1},{1... | collective-permute-start | bytes 1474568 | tf_op jit(solution)/shard_map/ppermute | solution.py:214
  105.8 6.2 %collective-permute-start.18 = (bf16[192,640]{1,0:T(8,128)(2,1)S(1)}, bf16[192,640]{1,0:T(8,128)(2,1)S(1)}, u32[]{:S(2)}, u32[]{:S(2)}) collective-permute-start(bf16[192,640]{1,0:T(8,128)(2,1)S(1)} %get-tuple-element.42.upper_ref), channel_id=1, source_target_pairs={{0,8},{1,5},{2,10},{3,7},{4,0},{5,13},{6,2},{7,15},{8,16},{9,1},{1... | collective-permute-start | bytes 737288 | tf_op jit(solution)/shard_map/ppermute | solution.py:222
  107.4 7.3 %collective-permute-start.25 = (bf16[192,640]{1,0:T(8,128)(2,1)S(1)}, bf16[192,640]{1,0:T(8,128)(2,1)S(1)}, u32[]{:S(2)}, u32[]{:S(2)}) collective-permute-start(bf16[192,640]{1,0:T(8,128)(2,1)S(1)} %get-tuple-element.41.lower_ref), channel_id=1, source_target_pairs={{0,8},{1,5},{2,10},{3,7},{4,0},{5,13},{6,2},{7,15},{8,16},{9,1},{1... | collective-permute-start | bytes 737288 | tf_op jit(solution)/shard_map/ppermute | solution.py:223
  112.1 6.2 %collective-permute-start.19 = (bf16[192,640]{1,0:T(8,128)(2,1)S(1)}, bf16[192,640]{1,0:T(8,128)(2,1)S(1)}, u32[]{:S(2)}, u32[]{:S(2)}) collective-permute-start(bf16[192,640]{1,0:T(8,128)(2,1)S(1)} %collective-permute-done.18.upper_ref), channel_id=1, source_target_pairs={{0,8},{1,5},{2,10},{3,7},{4,0},{5,13},{6,2},{7,15},{8,16},{9,1},{1... | collective-permute-start | bytes 737288 | tf_op jit(solution)/shard_map/ppermute | solution.py:222
  114.7 6.2 %collective-permute-start.26 = (bf16[192,640]{1,0:T(8,128)(2,1)S(1)}, bf16[192,640]{1,0:T(8,128)(2,1)S(1)}, u32[]{:S(2)}, u32[]{:S(2)}) collective-permute-start(bf16[192,640]{1,0:T(8,128)(2,1)S(1)} %collective-permute-done.25.lower_ref), channel_id=1, source_target_pairs={{0,8},{1,5},{2,10},{3,7},{4,0},{5,13},{6,2},{7,15},{8,16},{9,1},{1... | collective-permute-start | bytes 737288 | tf_op jit(solution)/shard_map/ppermute | solution.py:223
  118.3 6.2 %collective-permute-start.20 = (bf16[192,640]{1,0:T(8,128)(2,1)S(1)}, bf16[192,640]{1,0:T(8,128)(2,1)S(1)}, u32[]{:S(2)}, u32[]{:S(2)}) collective-permute-start(bf16[192,640]{1,0:T(8,128)(2,1)S(1)} %collective-permute-done.19.upper_ref), channel_id=1, source_target_pairs={{0,8},{1,5},{2,10},{3,7},{4,0},{5,13},{6,2},{7,15},{8,16},{9,1},{1... | collective-permute-start | bytes 737288 | tf_op jit(solution)/shard_map/ppermute | solution.py:222
  120.9 6.2 %collective-permute-start.27 = (bf16[192,640]{1,0:T(8,128)(2,1)S(1)}, bf16[192,640]{1,0:T(8,128)(2,1)S(1)}, u32[]{:S(2)}, u32[]{:S(2)}) collective-permute-start(bf16[192,640]{1,0:T(8,128)(2,1)S(1)} %collective-permute-done.26.lower_ref), channel_id=1, source_target_pairs={{0,8},{1,5},{2,10},{3,7},{4,0},{5,13},{6,2},{7,15},{8,16},{9,1},{1... | collective-permute-start | bytes 737288 | tf_op jit(solution)/shard_map/ppermute | solution.py:223
  124.5 6.2 %collective-permute-start.21 = (bf16[192,640]{1,0:T(8,128)(2,1)S(1)}, bf16[192,640]{1,0:T(8,128)(2,1)S(1)}, u32[]{:S(2)}, u32[]{:S(2)}) collective-permute-start(bf16[192,640]{1,0:T(8,128)(2,1)S(1)} %collective-permute-done.20.upper_ref), channel_id=1, source_target_pairs={{0,8},{1,5},{2,10},{3,7},{4,0},{5,13},{6,2},{7,15},{8,16},{9,1},{1... | collective-permute-start | bytes 737288 | tf_op jit(solution)/shard_map/ppermute | solution.py:222
  127.1 6.2 %collective-permute-start.28 = (bf16[192,640]{1,0:T(8,128)(2,1)S(1)}, bf16[192,640]{1,0:T(8,128)(2,1)S(1)}, u32[]{:S(2)}, u32[]{:S(2)}) collective-permute-start(bf16[192,640]{1,0:T(8,128)(2,1)S(1)} %collective-permute-done.27.lower_ref), channel_id=1, source_target_pairs={{0,8},{1,5},{2,10},{3,7},{4,0},{5,13},{6,2},{7,15},{8,16},{9,1},{1... | collective-permute-start | bytes 737288 | tf_op jit(solution)/shard_map/ppermute | solution.py:223
  130.7 6.2 %collective-permute-start.22 = (bf16[192,640]{1,0:T(8,128)(2,1)S(1)}, bf16[192,640]{1,0:T(8,128)(2,1)S(1)}, u32[]{:S(2)}, u32[]{:S(2)}) collective-permute-start(bf16[192,640]{1,0:T(8,128)(2,1)S(1)} %collective-permute-done.21.upper_ref), channel_id=1, source_target_pairs={{0,8},{1,5},{2,10},{3,7},{4,0},{5,13},{6,2},{7,15},{8,16},{9,1},{1... | collective-permute-start | bytes 737288 | tf_op jit(solution)/shard_map/ppermute | solution.py:222
  133.3 6.2 %collective-permute-start.29 = (bf16[192,640]{1,0:T(8,128)(2,1)S(1)}, bf16[192,640]{1,0:T(8,128)(2,1)S(1)}, u32[]{:S(2)}, u32[]{:S(2)}) collective-permute-start(bf16[192,640]{1,0:T(8,128)(2,1)S(1)} %collective-permute-done.28.lower_ref), channel_id=1, source_target_pairs={{0,8},{1,5},{2,10},{3,7},{4,0},{5,13},{6,2},{7,15},{8,16},{9,1},{1... | collective-permute-start | bytes 737288 | tf_op jit(solution)/shard_map/ppermute | solution.py:223
  136.9 6.2 %collective-permute-start.23 = (bf16[192,640]{1,0:T(8,128)(2,1)S(1)}, bf16[192,640]{1,0:T(8,128)(2,1)S(1)}, u32[]{:S(2)}, u32[]{:S(2)}) collective-permute-start(bf16[192,640]{1,0:T(8,128)(2,1)S(1)} %collective-permute-done.22.upper_ref), channel_id=1, source_target_pairs={{0,8},{1,5},{2,10},{3,7},{4,0},{5,13},{6,2},{7,15},{8,16},{9,1},{1... | collective-permute-start | bytes 737288 | tf_op jit(solution)/shard_map/ppermute | solution.py:222
  139.5 6.2 %collective-permute-start.30 = (bf16[192,640]{1,0:T(8,128)(2,1)S(1)}, bf16[192,640]{1,0:T(8,128)(2,1)S(1)}, u32[]{:S(2)}, u32[]{:S(2)}) collective-permute-start(bf16[192,640]{1,0:T(8,128)(2,1)S(1)} %collective-permute-done.29.lower_ref), channel_id=1, source_target_pairs={{0,8},{1,5},{2,10},{3,7},{4,0},{5,13},{6,2},{7,15},{8,16},{9,1},{1... | collective-permute-start | bytes 737288 | tf_op jit(solution)/shard_map/ppermute | solution.py:223
  143.1 18.9 %collective-permute-start.24 = (bf16[192,640]{1,0:T(8,128)(2,1)S(1)}, bf16[192,640]{1,0:T(8,128)(2,1)}, u32[]{:S(2)}, u32[]{:S(2)}) collective-permute-start(bf16[192,640]{1,0:T(8,128)(2,1)S(1)} %collective-permute-done.23.upper_ref), channel_id=1, source_target_pairs={{0,8},{1,5},{2,10},{3,7},{4,0},{5,13},{6,2},{7,15},{8,16},{9,1},{1... | collective-permute-start | bytes 737288 | tf_op jit(solution)/shard_map/ppermute | solution.py:222
  145.7 16.2 %collective-permute-start.31 = (bf16[192,640]{1,0:T(8,128)(2,1)S(1)}, bf16[192,640]{1,0:T(8,128)(2,1)}, u32[]{:S(2)}, u32[]{:S(2)}) collective-permute-start(bf16[192,640]{1,0:T(8,128)(2,1)S(1)} %collective-permute-done.30.lower_ref), channel_id=1, source_target_pairs={{0,8},{1,5},{2,10},{3,7},{4,0},{5,13},{6,2},{7,15},{8,16},{9,1},{1... | collective-permute-start | bytes 737288 | tf_op jit(solution)/shard_map/ppermute | solution.py:223
  165.2 4.9 %collective-permute-start.33 = (bf16[1,128,384]{2,1,0:T(8,128)(2,1)S(1)}, bf16[1,128,384]{2,1,0:T(8,128)(2,1)S(1)}, u32[]{:S(2)}, u32[]{:S(2)}) collective-permute-start(bf16[1,128,384]{2,1,0:T(8,128)(2,1)S(1)} %dynamic-slice_convert_fusion), channel_id=1, source_target_pairs={{0,2},{1,3},{2,0},{3,1},{4,6},{5,7},{6,4},{7,5},{8,10},{9,11},{10,... | collective-permute-start | bytes 294920 | tf_op jit(solution)/shard_map/ppermute | solution.py:233
  (2 other events, 4.0 us)
